TPU v7x, 256 devices: a whole 4x4x8 slice. The times are simulated.
256 devices in a mesh: term: 8 (over y, core), pass: 32 (over x, z).
Axes of the slice: x: 4, y: 4, z: 8, core: 2. Of those that a mesh axis runs over, the one named last changes fastest.
Arguments:
- hidden: bfloat16 [16384, 4096], P('pass', 'term'), may hold values from -16 to 16
- head_weight: bfloat16 [4096, 16384], P('pass', 'term'), may hold values from -0.09375 to 0.09375
- lengths: int32 [256], P('pass'), may hold values from 1 to 64, as said below
Outputs:
- postings: bfloat16 [16384, 256], P(('term', 'pass'))
Inputs may be any that keep to these rules, and one draw needn't show every extreme that they name: Passage p's valid tokens are its first lengths[p] slots; some passage has exactly 64.
All inputs are finite; a program needn't handle non-finite values.
Results may differ from a plain program's by a relative error of at most 0.013.
Values may be sent and summed in bfloat16 or wider, within the bound.
No kernel may reach another device: no remote copies, remote signals or barrier semaphores. Data moves between devices by JAX's collectives and lax.ppermute only.
A program may use at most 64 MiB of HBM per device.

v0:
```python
import jax
import jax.numpy as jnp
from jax import lax
from jax.sharding import PartitionSpec as P


def body(hidden, head_weight, lengths):
    gathered = lax.all_gather(hidden, "term", axis=1, tiled=True)
    passages = lengths.shape[0]
    tokens_per = gathered.shape[0] // passages
    slab_cols = head_weight.shape[1]
    allowed = jnp.arange(tokens_per, dtype=jnp.int32)[None, :] < lengths[:, None]
    logits = jnp.dot(
        gathered,
        lax.all_gather(head_weight, "pass", axis=0, tiled=True),
        preferred_element_type=jnp.float32,
    )
    impacts = jnp.log1p(jnp.maximum(logits, jnp.float32(0.0)))
    impacts = impacts.reshape(passages, tokens_per, slab_cols)
    impacts = jnp.where(allowed[:, :, None], impacts, jnp.float32(0.0))
    pooled = jnp.max(impacts, axis=1).astype(jnp.bfloat16)
    owners = lax.axis_size("pass")
    range_cols = slab_cols // owners
    local_max = jnp.max(pooled.astype(jnp.float32), axis=0)
    column_max = lax.pmax(local_max, "pass")
    payload = (pooled.astype(jnp.float32) / (1.0 + column_max)[None, :]).astype(jnp.bfloat16)
    shaped = payload.reshape(passages, owners, range_cols)
    return jnp.transpose(
        lax.all_to_all(shaped, "pass", split_axis=1, concat_axis=0, tiled=True)[:, 0, :]
    )


def solution(mesh):
    return jax.shard_map(
        body,
        mesh=mesh,
        in_specs=(P("pass", "term"), P("pass", "term"), P("pass")),
        out_specs=P(("term", "pass"), None),
        check_vma=False,
    )
```

profile of v0, /device:TPU:8, one launch (start us, length us, event | category | flops | bytes accessed | tf_op | source)
XLA Modules:
  0.0 297.9 jit_solution(6542916140701454250)
XLA Ops:
  6.5 0.0 all-gather.3.cloned.1.call-start
  6.5 0.7 all-gather.3.cloned.1.call-update
  7.3 0.0 all-gather.5.cloned.1.call-start
  7.3 0.7 all-gather.5.cloned.1.call-update
  8.0 0.7 iota_compare_fusion
  8.7 37.0 %all-gather.3.cloned.1.call-done = bf16[512,4096]{1,0:T(8,128)(2,1)} async-done(((bf16[512,512]{1,0:T(8,128)(2,1)}), bf16[512,4096]{1,0:T(8,128)(2,1)}) %all-gather.3.cloned.1.call-update) | async-done | bytes 4194320 | tf_op jit(solution)/shard_map/all_gather | solution.py:8
  45.8 144.1 %all-gather.5.cloned.1.call-done = bf16[4096,2048]{1,0:T(8,128)(2,1)} async-done(((bf16[128,2048]{1,0:T(8,128)(2,1)}), bf16[4096,2048]{1,0:T(8,128)(2,1)}) %all-gather.5.cloned.1.call-update) | async-done | bytes 16777232 | tf_op jit(solution)/shard_map/all_gather | solution.py:15
  189.9 14.8 %select_reduce_fusion = bf16[8,2048]{1,0:T(8,128)(2,1)S(1)} fusion(pred[8,64]{1,0:T(8,128)(4,1)S(1)} %iota_compare_fusion, bf16[512,4096]{1,0:T(8,128)(2,1)} %all-gather.3.cloned.1.call-done, bf16[4096,2048]{1,0:T(8,128)(2,1)} %all-gather.5.cloned.1.call-done), kind=kOutput, calls=%fused_computation | convolution fusion | flops 8594112512 | bytes 21004800 | tf_op jit(solution)/shard_map/dot_general | solution.py:13
  204.8 0.1 reshape.37
  204.9 72.3 %pmax.7 = f32[2048]{0:T(1024)S(1)} all-reduce(bf16[2048]{0:T(1024)(128)(2,1)S(1)} %convert_reduce_fusion), channel_id=1, replica_groups=mesh['term'=8,'pass'=32] {'pass'}, use_global_device_ids=true, to_apply=%region_2.3 | all-reduce | flops 2048 | bytes 12288 | tf_op jit(solution)/shard_map/pmax | solution.py:25
  277.2 0.1 div.11
  277.3 0.1 reshape.38
  277.4 12.8 %all_to_all.15 = bf16[32,2,256]{2,1,0:T(2,128)(2,1)S(1)} all-to-all(bf16[32,2,256]{2,1,0:T(2,128)(2,1)S(1)} %reshape.38), channel_id=1, replica_groups=mesh['term'=8,'pass'=32] {'pass'}, dimensions={0} | all-to-all | bytes 65536 | tf_op jit(solution)/shard_map/all_to_all | solution.py:29
  290.2 0.1 reshape.39
  290.4 0.7 copy.7
  (5 shorter events, 0.1 us)
Async XLA Ops:
  6.5 39.2 %all-gather.3.cloned.1.call-start = ((), (), s32[]{:S(2)}) async-start(), calls=%async_computation.1 | async-start | bytes 4718592 | tf_op jit(solution)/shard_map/all_gather | solution.py:8
  7.3 182.6 %all-gather.5.cloned.1.call-start = ((), (), s32[]{:S(2)}) async-start(), calls=%async_computation.2 | async-start | bytes 17301504 | tf_op jit(solution)/shard_map/all_gather | solution.py:15
Sparse Core Ops, SparseCore 0:
  9.2 36.5 all-gather.2
  48.4 141.4 all-gather.4
where the time goes:
time: 298 us
  waiting for transfers between devices  183 us (61%)
  blocking collectives  85.1 us (29%)
  matrix products  14.8 us (5%)
  between operations  13.5 us (5%)
    all_gather x1, waiting for transfers between devices, body(): lax.all_gather(head_weight, 'pass', axis=0, tiled=True)  144 us
    pmax x1, blocking collectives, body(): column_max = lax.pmax(local_max, 'pass')  72.3 us
    all_gather x1, waiting for transfers between devices, body(): gathered = lax.all_gather(hidden, 'term', axis=1, tiled=True)  37 us
    dot_general x1, matrix products, body(): jnp.dot(gathered, lax.all_gather(head_weight, 'pass', axis=0, tiled=True)...  14.8 us
    all_to_all x1, blocking collectives, body(): lax.all_to_all(shaped, 'pass', split_axis=1, concat_axis=0, tiled=True)  12.8 us
  transfers between devices with their start and end apart: 2, of which 2 were waited for; matrix products, arithmetic and copies ran while one was open for 0% of the time, Pallas kernels for 0%

commit v1 on v0

--- a/solution.py
+++ b/solution.py
@@ -5,7 +5,12 @@
 
 
 def body(hidden, head_weight, lengths):
-    gathered = lax.all_gather(hidden, "term", axis=1, tiled=True)
+    ring = [hidden]
+    for hop in range(7):
+        ring.append(lax.ppermute(ring[-1], "term", [(dev, (dev + 1) % 8) for dev in range(8)]))
+    gathered = jnp.roll(
+        jnp.concatenate(ring[::-1], axis=1), (lax.axis_index("term") + 1) * ring[0].shape[1], axis=1
+    )
     passages = lengths.shape[0]
     tokens_per = gathered.shape[0] // passages
     slab_cols = head_weight.shape[1]

time: 298 us -> 262 us (0.88)
  waiting for transfers between devices: 183 us -> 127 us
  local copies, waits for them, and re-layouts: 1.16 us -> 20.6 us
    all_gather x1, waiting for transfers between devices: 144 us -> 65.7 us  [body(): lax.all_gather(head_weight, 'pass', axis=0, tiled=True)]
    ppermute x0 -> x7, waiting for transfers between devices: none -> 60.1 us  [body(): lax.ppermute(ring[-1], 'term', [(dev, (dev + 1) % 8) for dev in range(8)])]
    all_gather x1 -> x0, waiting for transfers between devices: 37 us -> none  [body(): gathered = lax.all_gather(hidden, 'term', axis=1, tiled=True)]
    unnamed x2 -> x19, local copies, waits for them, and re-layouts: 0.22 us -> 18.8 us
  transfers between devices with their start and end apart: 2 -> 8, of which waited for: 2 -> 8; matrix products, arithmetic and copies ran while one was open for 0% -> 8% of each run, Pallas kernels for 0% -> 0%
where the time goes in v1:
time: 262 us; the launch traced here: 261 us
  waiting for transfers between devices  127 us (48%)
  blocking collectives  85.1 us (32%)
  local copies, waits for them, and re-layouts  20.6 us (8%)
  matrix products  14.8 us (6%)
  between operations  13.5 us (5%)
    pmax x1, blocking collectives, body(): column_max = lax.pmax(local_max, 'pass')  72.3 us
    all_gather x1, waiting for transfers between devices, body(): lax.all_gather(head_weight, 'pass', axis=0, tiled=True)  65.7 us
    ppermute x7, waiting for transfers between devices, body(): lax.ppermute(ring[-1], 'term', [(dev, (dev + 1) % 8) for dev in range(8)])  60.1 us
    unnamed x19, local copies, waits for them, and re-layouts  18.8 us
    dot_general x1, matrix products, body(): jnp.dot(gathered, lax.all_gather(head_weight, 'pass', axis=0, tiled=True)...  14.8 us
    all_to_all x1, blocking collectives, body(): lax.all_to_all(shaped, 'pass', split_axis=1, concat_axis=0, tiled=True)  12.8 us
  transfers between devices with their start and end apart: 8, of which 8 were waited for; matrix products, arithmetic and copies ran while one was open for 8% of the time, Pallas kernels for 0%

profile of v1, /device:TPU:8, one launch (start us, length us, event | category | flops | bytes accessed | tf_op | source)
XLA Modules:
  0.0 261.4 jit_solution(5148266944038984518)
XLA Ops:
  6.5 0.7 all-gather.2.cloned.1.call-update
  7.3 8.8 %collective-permute-done = bf16[512,512]{1,0:T(8,128)(2,1)S(1)} collective-permute-done((bf16[512,512]{1,0:T(8,128)(2,1)}, bf16[512,512]{1,0:T(8,128)(2,1)S(1)}, u32[]{:S(2)}, u32[]{:S(2)}) %collective-permute-start) | collective-permute-done | bytes 524320 | tf_op jit(solution)/shard_map/ppermute | solution.py:10
  16.1 8.6 %collective-permute-done.1 = bf16[512,512]{1,0:T(8,128)(2,1)S(1)} collective-permute-done((bf16[512,512]{1,0:T(8,128)(2,1)S(1)}, bf16[512,512]{1,0:T(8,128)(2,1)S(1)}, u32[]{:S(2)}, u32[]{:S(2)}) %collective-permute-start.1) | collective-permute-done | bytes 524320 | tf_op jit(solution)/shard_map/ppermute | solution.py:10
  24.7 8.6 %collective-permute-done.2 = bf16[512,512]{1,0:T(8,128)(2,1)S(1)} collective-permute-done((bf16[512,512]{1,0:T(8,128)(2,1)S(1)}, bf16[512,512]{1,0:T(8,128)(2,1)S(1)}, u32[]{:S(2)}, u32[]{:S(2)}) %collective-permute-start.2) | collective-permute-done | bytes 524320 | tf_op jit(solution)/shard_map/ppermute | solution.py:10
  33.3 8.6 %collective-permute-done.3 = bf16[512,512]{1,0:T(8,128)(2,1)S(1)} collective-permute-done((bf16[512,512]{1,0:T(8,128)(2,1)S(1)}, bf16[512,512]{1,0:T(8,128)(2,1)S(1)}, u32[]{:S(2)}, u32[]{:S(2)}) %collective-permute-start.3) | collective-permute-done | bytes 524320 | tf_op jit(solution)/shard_map/ppermute | solution.py:10
  41.9 8.6 %collective-permute-done.4 = bf16[512,512]{1,0:T(8,128)(2,1)S(1)} collective-permute-done((bf16[512,512]{1,0:T(8,128)(2,1)S(1)}, bf16[512,512]{1,0:T(8,128)(2,1)S(1)}, u32[]{:S(2)}, u32[]{:S(2)}) %collective-permute-start.4) | collective-permute-done | bytes 524320 | tf_op jit(solution)/shard_map/ppermute | solution.py:10
  50.5 8.7 %collective-permute-done.5 = bf16[512,512]{1,0:T(8,128)(2,1)} collective-permute-done((bf16[512,512]{1,0:T(8,128)(2,1)S(1)}, bf16[512,512]{1,0:T(8,128)(2,1)}, u32[]{:S(2)}, u32[]{:S(2)}) %collective-permute-start.5) | collective-permute-done | bytes 524320 | tf_op jit(solution)/shard_map/ppermute | solution.py:10
  59.2 0.7 iota_compare_fusion
  60.0 8.2 %collective-permute-done.6 = bf16[512,512]{1,0:T(8,128)(2,1)} collective-permute-done((bf16[512,512]{1,0:T(8,128)(2,1)}, bf16[512,512]{1,0:T(8,128)(2,1)}, u32[]{:S(2)}, u32[]{:S(2)}) %collective-permute-start.6) | collective-permute-done | bytes 524320 | tf_op jit(solution)/shard_map/ppermute | solution.py:10
  68.1 2.0 constant_dynamic-update-slice_fusion.15
  70.2 1.9 constant_dynamic-update-slice_fusion.14
  72.1 0.8 constant_dynamic-update-slice_fusion.13
  72.9 0.9 constant_dynamic-update-slice_fusion.12
  73.8 0.9 constant_dynamic-update-slice_fusion.11
  74.6 0.8 constant_dynamic-update-slice_fusion.10
  75.5 0.9 constant_dynamic-update-slice_fusion.9
  76.3 1.9 constant_dynamic-update-slice_fusion.8
  78.3 1.9 constant_dynamic-update-slice_fusion.7
  80.2 1.9 constant_dynamic-update-slice_fusion.6
  82.1 0.9 constant_dynamic-update-slice_fusion.5
  83.0 0.9 constant_dynamic-update-slice_fusion.4
  84.0 0.9 constant_dynamic-update-slice_fusion.3
  84.8 1.0 constant_dynamic-update-slice_fusion.2
  85.8 0.9 constant_dynamic-update-slice_fusion.1
  86.7 0.9 constant_dynamic-update-slice_fusion
  87.6 65.7 %all-gather.2.cloned.1.call-done = bf16[4096,2048]{1,0:T(8,128)(2,1)} async-done(((bf16[128,2048]{1,0:T(8,128)(2,1)}), bf16[4096,2048]{1,0:T(8,128)(2,1)}) %all-gather.2.cloned.1.call-update) | async-done | bytes 16777232 | tf_op jit(solution)/shard_map/all_gather | solution.py:20
  153.4 14.8 %select_reduce_fusion = bf16[8,2048]{1,0:T(8,128)(2,1)S(1)} fusion(pred[8,64]{1,0:T(8,128)(4,1)S(1)} %iota_compare_fusion, bf16[4096,2048]{1,0:T(8,128)(2,1)} %all-gather.2.cloned.1.call-done, bf16[512,8192]{1,0:T(8,128)(2,1)} %constant_dynamic-update-slice_fusion, s32[]{:T(128)S(6)} %select_n.18), kind=kOutput, calls=%fused_computation | convolution fusion | flops 8594112512 | bytes 21004804 | tf_op jit(solution)/shard_map/dot_general | solution.py:18
  168.2 0.1 reshape.37
  168.3 72.3 %pmax.7 = f32[2048]{0:T(1024)S(1)} all-reduce(bf16[2048]{0:T(1024)(128)(2,1)S(1)} %convert_reduce_fusion), channel_id=1, replica_groups=mesh['term'=8,'pass'=32] {'pass'}, use_global_device_ids=true, to_apply=%region_2.3 | all-reduce | flops 2048 | bytes 12288 | tf_op jit(solution)/shard_map/pmax | solution.py:30
  240.8 0.1 reshape.38
  240.9 12.8 %all_to_all.15 = bf16[32,2,256]{2,1,0:T(2,128)(2,1)S(1)} all-to-all(bf16[32,2,256]{2,1,0:T(2,128)(2,1)S(1)} %reshape.38), channel_id=1, replica_groups=mesh['term'=8,'pass'=32] {'pass'}, dimensions={0} | all-to-all | bytes 65536 | tf_op jit(solution)/shard_map/all_to_all | solution.py:34
  253.8 0.7 copy.7
  (17 shorter events, 0.3 us)
Async XLA Ops:
  6.5 80.2 %copy-start = (bf16[512,512]{1,0:T(8,128)(2,1)S(1)}, bf16[512,512]{1,0:T(8,128)(2,1)}, u32[]{:S(2)}) copy-start(bf16[512,512]{1,0:T(8,128)(2,1)} %param.3) | copy-start | bytes 1572868
  6.5 146.8 %all-gather.2.cloned.1.call-start = ((), (), s32[]{:S(2)}) async-start(), calls=%async_computation.1 | async-start | bytes 17301504 | tf_op jit(solution)/shard_map/all_gather | solution.py:20
  7.3 8.8 %collective-permute-start = (bf16[512,512]{1,0:T(8,128)(2,1)}, bf16[512,512]{1,0:T(8,128)(2,1)S(1)}, u32[]{:S(2)}, u32[]{:S(2)}) collective-permute-start(bf16[512,512]{1,0:T(8,128)(2,1)} %param.3), channel_id=1, source_target_pairs={{0,32},{32,64},{64,96},{96,128},{128,160},{160,192},{192,224},{224... | collective-permute-start | bytes 1572872 | tf_op jit(solution)/shard_map/ppermute | solution.py:10
  16.1 8.6 %collective-permute-start.1 = (bf16[512,512]{1,0:T(8,128)(2,1)S(1)}, bf16[512,512]{1,0:T(8,128)(2,1)S(1)}, u32[]{:S(2)}, u32[]{:S(2)}) collective-permute-start(bf16[512,512]{1,0:T(8,128)(2,1)S(1)} %collective-permute-done), channel_id=1, source_target_pairs={{0,32},{32,64},{64,96},{96,128},{128,160},{160,192},{192,224},{224... | collective-permute-start | bytes 1572872 | tf_op jit(solution)/shard_map/ppermute | solution.py:10
  24.7 8.6 %collective-permute-start.2 = (bf16[512,512]{1,0:T(8,128)(2,1)S(1)}, bf16[512,512]{1,0:T(8,128)(2,1)S(1)}, u32[]{:S(2)}, u32[]{:S(2)}) collective-permute-start(bf16[512,512]{1,0:T(8,128)(2,1)S(1)} %collective-permute-done.1), channel_id=1, source_target_pairs={{0,32},{32,64},{64,96},{96,128},{128,160},{160,192},{192,224},{224... | collective-permute-start | bytes 1572872 | tf_op jit(solution)/shard_map/ppermute | solution.py:10
  33.3 8.6 %collective-permute-start.3 = (bf16[512,512]{1,0:T(8,128)(2,1)S(1)}, bf16[512,512]{1,0:T(8,128)(2,1)S(1)}, u32[]{:S(2)}, u32[]{:S(2)}) collective-permute-start(bf16[512,512]{1,0:T(8,128)(2,1)S(1)} %collective-permute-done.2), channel_id=1, source_target_pairs={{0,32},{32,64},{64,96},{96,128},{128,160},{160,192},{192,224},{224... | collective-permute-start | bytes 1572872 | tf_op jit(solution)/shard_map/ppermute | solution.py:10
  41.9 8.6 %collective-permute-start.4 = (bf16[512,512]{1,0:T(8,128)(2,1)S(1)}, bf16[512,512]{1,0:T(8,128)(2,1)S(1)}, u32[]{:S(2)}, u32[]{:S(2)}) collective-permute-start(bf16[512,512]{1,0:T(8,128)(2,1)S(1)} %collective-permute-done.3), channel_id=1, source_target_pairs={{0,32},{32,64},{64,96},{96,128},{128,160},{160,192},{192,224},{224... | collective-permute-start | bytes 1572872 | tf_op jit(solution)/shard_map/ppermute | solution.py:10
  50.5 8.7 %collective-permute-start.5 = (bf16[512,512]{1,0:T(8,128)(2,1)S(1)}, bf16[512,512]{1,0:T(8,128)(2,1)}, u32[]{:S(2)}, u32[]{:S(2)}) collective-permute-start(bf16[512,512]{1,0:T(8,128)(2,1)S(1)} %collective-permute-done.4), channel_id=1, source_target_pairs={{0,32},{32,64},{64,96},{96,128},{128,160},{160,192},{192,224},{224... | collective-permute-start | bytes 1572872 | tf_op jit(solution)/shard_map/ppermute | solution.py:10
  59.2 8.9 %collective-permute-start.6 = (bf16[512,512]{1,0:T(8,128)(2,1)}, bf16[512,512]{1,0:T(8,128)(2,1)}, u32[]{:S(2)}, u32[]{:S(2)}) collective-permute-start(bf16[512,512]{1,0:T(8,128)(2,1)} %collective-permute-done.5), channel_id=1, source_target_pairs={{0,32},{32,64},{64,96},{96,128},{128,160},{160,192},{192,224},{224... | collective-permute-start | bytes 1572872 | tf_op jit(solution)/shard_map/ppermute | solution.py:10
Sparse Core Ops, SparseCore 0:
  9.9 143.3 all-gather.1
